TPU v7x, 256 devices: a whole 4x4x8 slice. The times are simulated.
256 devices in a mesh: seq: 64 (over y, z, core), mp: 4 (over x).
Axes of the slice: x: 4, y: 4, z: 8, core: 2. Of those that a mesh axis runs over, the one named last changes fastest.
Arguments:
- tokens: bfloat16 [8192, 3584], P('seq'), may hold values from -6 to 6
- query_weight: bfloat16 [3584, 4096], P('seq', 'mp'), may hold values from -0.09375 to 0.09375
- key_weight: bfloat16 [3584, 4096], P('seq', 'mp'), may hold values from -0.09375 to 0.09375
- value_weight: bfloat16 [3584, 4096], P('seq', 'mp'), may hold values from -0.09375 to 0.09375
- adapter_down_maps: bfloat16 [3584, 128], replicated, may hold values from -0.09375 to 0.09375
- lifting_matrices: bfloat16 [2, 64, 4096], P(None, None, 'mp'), may hold values from -0.75 to 0.75
- decay_logarithms: float32 [32, 8192], P('mp', 'seq'), may hold values from -1 to 0, as said below
- output_gradient: bfloat16 [8192, 4096], P('seq', 'mp'), may hold values from -0.06591797 to 0.06591797
Outputs:
- grad_down: float32 [3584, 128], P(('seq', 'mp'))
- grad_up: float32 [2, 64, 4096], P(None, None, 'mp')
Inputs may be any that keep to these rules, and one draw needn't show every extreme that they name: `decay_logarithms`: every entry is negative.
All inputs are finite; a program needn't handle non-finite values.
Results may differ from a plain program's by a relative error of at most 0.006.
Values may be sent and summed in bfloat16 or wider, within the bound.
No kernel may reach another device: no remote copies, remote signals or barrier semaphores. Data moves between devices by JAX's collectives and lax.ppermute only.
A program may use at most 192 MiB of HBM per device.

v0:
```python
import jax
import jax.numpy as jnp
from jax import lax
from jax.sharding import PartitionSpec as P

adapter_scale = 2.0
eps_norm = 1e-06
exact_arithmetic = lax.Precision.HIGHEST


def carried_in(value, axis, join, neutral, backward):
    count, mine = (lax.axis_size(axis), lax.axis_index(axis))
    pieces = jax.tree.map(lambda part: lax.all_gather(part, axis), value)
    if backward:
        pieces = jax.tree.map(lambda part: part[::-1], pieces)
        mine = count - 1 - mine
    so_far = jax.tree.map(
        lambda part, zero: jnp.full_like(part, 0) + jnp.asarray(zero, part.dtype), value, neutral
    )

    def hop(position, so_far):
        longer = join(so_far, jax.tree.map(lambda part: part[position], pieces))
        return jax.tree.map(lambda new, old: jnp.where(position < mine, new, old), longer, so_far)

    return lax.fori_loop(0, count - 1, hop, so_far)


def combine(earlier, later):
    return (earlier[0] * later[0], later[0][:, None, None] * earlier[1] + later[1])


def split_heads(flat, heads):
    return flat.reshape(flat.shape[0], heads, flat.shape[1] // heads).transpose(1, 0, 2)


def join_heads(arr):
    return arr.transpose(1, 0, 2).reshape(arr.shape[1], arr.shape[0] * arr.shape[2])


def on_device(
    tokens,
    query_weight,
    key_weight,
    value_weight,
    adapter_down_maps,
    lifting_matrices,
    decay_logarithms,
    output_gradient,
):
    length = tokens.shape[0]
    heads = decay_logarithms.shape[0]
    rank_index = lifting_matrices.shape[1]
    low_product = jnp.dot(tokens, adapter_down_maps, preferred_element_type=jnp.float32).astype(
        jnp.bfloat16
    )
    query_low_product = low_product[:, :rank_index]
    value_low_product = low_product[:, rank_index:]
    cumulative = jnp.cumsum(decay_logarithms, axis=1)
    total = cumulative[:, -1]
    gain = jnp.exp(total)
    tail = jnp.exp(total[:, None] - cumulative)
    lead = jnp.exp(cumulative)
    causal = jnp.arange(length)[:, None] >= jnp.arange(length)[None, :]
    spread = cumulative[:, :, None] - cumulative[:, None, :]
    decay_mat = jnp.where(causal[None], jnp.exp(jnp.where(causal[None], spread, 0.0)), 0.0)
    pieces = (
        lax.all_gather(query_weight, "seq", axis=0, tiled=True),
        lax.all_gather(key_weight, "seq", axis=0, tiled=True),
        lax.all_gather(value_weight, "seq", axis=0, tiled=True),
    )
    columns = tokens
    query_frozen_part, key_base, value_frozen_part = tuple(
        (jnp.dot(columns, piece, preferred_element_type=jnp.float32) for piece in pieces)
    )
    value_before_norm = value_frozen_part + adapter_scale * jnp.dot(
        value_low_product, lifting_matrices[1], preferred_element_type=jnp.float32
    )
    key_heads = split_heads(jax.nn.silu(key_base).astype(jnp.bfloat16), heads)
    value_heads = split_heads(value_before_norm.astype(jnp.bfloat16), heads)
    key_f = key_heads.astype(jnp.float32)
    local = jnp.einsum(
        "hsi,hsj->hij",
        key_f * tail[:, :, None],
        value_heads.astype(jnp.float32),
        precision=exact_arithmetic,
    )
    state_in = carried_in(
        (gain, local), "seq", combine, (jnp.ones_like(gain), jnp.zeros_like(local)), False
    )[1]
    key_heads, key_f, value_heads, state_in = (key_heads, key_f, value_heads, state_in)
    query_before_norm = query_frozen_part + adapter_scale * jnp.dot(
        query_low_product, lifting_matrices[0], preferred_element_type=jnp.float32
    )
    query_heads = split_heads(jax.nn.silu(query_before_norm).astype(jnp.bfloat16), heads)
    query_f = query_heads.astype(jnp.float32)
    scores = jnp.einsum("htd,hsd->hts", query_heads, key_heads, preferred_element_type=jnp.float32)
    mixed = (scores * decay_mat).astype(jnp.bfloat16)
    attn = jnp.einsum(
        "hts,hsj->htj", mixed, value_heads, preferred_element_type=jnp.float32
    ) + lead[:, :, None] * jnp.einsum("hti,hij->htj", query_f, state_in, precision=exact_arithmetic)
    rms = jnp.sqrt(jnp.mean(attn * attn, axis=-1, keepdims=True) + eps_norm)
    normed = attn / rms
    upstream = split_heads(output_gradient, heads).astype(jnp.float32)
    d_attn = (upstream - normed * jnp.mean(upstream * normed, axis=-1, keepdims=True)) / rms
    d_attn_b = d_attn.astype(jnp.bfloat16)
    carried = jnp.einsum(
        "hti,htj->hij", query_f * lead[:, :, None], d_attn, precision=exact_arithmetic
    )
    later = carried_in(
        (gain, carried), "seq", combine, (jnp.ones_like(gain), jnp.zeros_like(carried)), True
    )[1]
    d_mixed = (
        jnp.einsum("htj,hsj->hts", d_attn_b, value_heads, preferred_element_type=jnp.float32)
        * decay_mat
    ).astype(jnp.bfloat16)
    d_query = jnp.einsum(
        "hts,hsi->hti", d_mixed, key_heads, preferred_element_type=jnp.float32
    ) + lead[:, :, None] * jnp.einsum("htj,hij->hti", d_attn, state_in, precision=exact_arithmetic)
    d_value = jnp.einsum(
        "hts,htj->hsj", mixed, d_attn_b, preferred_element_type=jnp.float32
    ) + tail[:, :, None] * jnp.einsum("hsi,hij->hsj", key_f, later, precision=exact_arithmetic)
    sig = jax.nn.sigmoid(query_before_norm)
    query_pre_gradient = join_heads(d_query) * (sig * (1.0 + query_before_norm * (1.0 - sig)))
    value_flat_gradient = join_heads(d_value)
    low_product_float = low_product.astype(jnp.float32)
    up_products = jnp.stack(
        [
            adapter_scale
            * jnp.dot(
                low_product_float[:, :rank_index].T, query_pre_gradient, precision=exact_arithmetic
            ),
            adapter_scale
            * jnp.dot(
                low_product_float[:, rank_index:].T, value_flat_gradient, precision=exact_arithmetic
            ),
        ]
    )
    grad_up = lax.psum(up_products, "seq")
    low_gradient = adapter_scale * jnp.concatenate(
        [
            jnp.dot(
                query_pre_gradient,
                lifting_matrices[0].astype(jnp.float32).T,
                precision=exact_arithmetic,
            ),
            jnp.dot(
                value_flat_gradient,
                lifting_matrices[1].astype(jnp.float32).T,
                precision=exact_arithmetic,
            ),
        ],
        axis=1,
    )
    columns = tokens.astype(jnp.float32)
    grad_down = lax.psum_scatter(
        jnp.dot(columns.T, low_gradient, precision=exact_arithmetic),
        ("seq", "mp"),
        scatter_dimension=0,
        tiled=True,
    )
    return (grad_down, grad_up)


def solution(mesh):
    return jax.shard_map(
        on_device,
        mesh=mesh,
        in_specs=(
            P("seq", None),
            P("seq", "mp"),
            P("seq", "mp"),
            P("seq", "mp"),
            P(),
            P(None, None, "mp"),
            P("mp", "seq"),
            P("seq", "mp"),
        ),
        out_specs=(P(("seq", "mp"), None), P(None, None, "mp")),
        check_vma=False,
    )
```

profile of v0, /device:TPU:2, one launch (start us, length us, event | category | flops | bytes accessed | tf_op | source)
XLA Modules:
  0.0 1261.7 jit_solution(11165250688478119228)
XLA Ops:
  10.7 1.7 convolution_convert_fusion
  12.4 83.2 %all-gather.13.cloned.1.call-done = bf16[3584,1024]{1,0:T(8,128)(2,1)} async-done(((bf16[56,1024]{1,0:T(8,128)(2,1)}), bf16[3584,1024]{1,0:T(8,128)(2,1)}) %all-gather.13.cloned.1.call-update) | async-done | bytes 7340048 | tf_op jit(solution)/shard_map/all_gather | solution.py:69
  95.5 4.2 fusion.57
  100.0 76.9 %all-gather.11.cloned.1.call-done = bf16[3584,1024]{1,0:T(8,128)(2,1)} async-done(((bf16[56,1024]{1,0:T(8,128)(2,1)}), bf16[3584,1024]{1,0:T(8,128)(2,1)}) %all-gather.11.cloned.1.call-update) | async-done | bytes 7340048 | tf_op jit(solution)/shard_map/all_gather | solution.py:68
  176.9 4.3 multiply_convert_fusion
  181.2 1.5 fusion.16
  184.2 127.0 %all-reduce = f32[512]{0:T(512)S(1)} all-reduce(f32[512]{0:T(512)S(1)} %dynamic-update-slice), channel_id=2, replica_groups=mesh['seq'=64,'mp'=4] {'seq'}, use_global_device_ids=true, to_apply=%add | all-reduce | flops 512 | bytes 4096
  313.5 4.3 fusion.56
  320.1 1.8 fusion.9
  321.8 78.4 %all-gather.15.cloned.1.call-done = f32[512,128,128]{2,1,0:T(8,128)} async-done(((f32[8,128,128]{2,1,0:T(8,128)}), f32[512,128,128]{2,1,0:T(8,128)}) %all-gather.15.cloned.1.call-update) | async-done | bytes 33554448 | tf_op jit(solution)/shard_map/all_gather | solution.py:13
  400.3 118.5 %while.28 = (s32[]{:T(128)}, f32[8,128,128]{2,1,0:T(8,128)S(1)}, s32[]{:T(128)}, f32[64,8]{1,0:T(8,128)}, f32[64,8,128,128]{3,2,1,0:T(8,128)}, /*index=5*/s32[]{:T(128)}, s32[]{:T(128)}) while((s32[]{:T(128)}, f32[8,128,128]{2,1,0:T(8,128)S(1)}, s32[]{:T(128)}, f32[64,8]{1,0:T(8,128)}, f32[64,8,128,128]{3,2,1,0:T(8,128)}, ...), condition=%wide.region_2.3_spmd.clone, body=%wide.region_1.2_spmd.clone.sunk | while | flops 524292 | bytes 1573073 | solution.py:25
  519.4 1.4 multiply_reduce_fusion.1
  520.9 2.0 fusion.13
  523.2 1.4 rev.6
  526.2 1.3 fusion.2
  527.6 1.2 multiply_multiply_fusion
  528.9 1.3 fusion.36
  530.2 131.7 %all-gather.17.cloned.1.call-done = f32[512,128,128]{2,1,0:T(8,128)} async-done(((f32[8,128,128]{2,1,0:T(8,128)}), f32[512,128,128]{2,1,0:T(8,128)}) %all-gather.17.cloned.1.call-update) | async-done | bytes 33554448 | tf_op jit(solution)/shard_map/all_gather | solution.py:13
  661.9 23.0 %rev.7 = f32[64,8,128,128]{3,2,1,0:T(8,128)} reverse(f32[64,8,128,128]{3,2,1,0:T(8,128)} %bitcast.144), dimensions={0} | reverse | bytes 67108864 | tf_op jit(solution)/shard_map/rev | solution.py:15
  684.9 118.6 %while.29 = (s32[]{:T(128)}, f32[8,128,128]{2,1,0:T(8,128)S(1)}, s32[]{:T(128)}, f32[64,8]{1,0:T(8,128)}, f32[64,8,128,128]{3,2,1,0:T(8,128)}, /*index=5*/s32[]{:T(128)}, s32[]{:T(128)}) while((s32[]{:T(128)}, f32[8,128,128]{2,1,0:T(8,128)S(1)}, s32[]{:T(128)}, f32[64,8]{1,0:T(8,128)}, f32[64,8,128,128]{3,2,1,0:T(8,128)}, ...), condition=%wide.region_6.7_spmd.clone, body=%wide.region_5.6_spmd.clone.sunk | while | flops 524292 | bytes 1573073 | solution.py:25
  804.6 2.1 convolution_bitcast_fusion
  808.5 258.2 %all-reduce.7.cloned.1.call-done = f32[3584,128]{0,1:T(8,128)} async-done(((f32[3584,128]{0,1:T(8,128)}), f32[3584,128]{0,1:T(8,128)}) %all-reduce.7.cloned.1.call-update) | async-done | bytes 1835024
  1068.3 184.6 %all-reduce.5.cloned.1.call-done = f32[2,64,1024]{2,1,0:T(8,128)} async-done(((f32[2,64,1024]{2,1,0:T(8,128)}), f32[2,64,1024]{2,1,0:T(8,128)}) %all-reduce.5.cloned.1.call-update) | async-done | bytes 524304 | tf_op jit(solution)/shard_map/psum | solution.py:138
  1252.9 1.9 copy.120
  (318 shorter events, 250.1 us)
Async XLA Ops:
  7.2 3.5 copy-start
  7.2 88.4 %all-gather.13.cloned.1.call-start = ((), (), s32[]{:S(2)}) async-start(), calls=%async_computation.2 | async-start | bytes 7454720 | tf_op jit(solution)/shard_map/all_gather | solution.py:69
  7.9 169.0 %all-gather.11.cloned.1.call-start = ((), (), s32[]{:S(2)}) async-start(), calls=%async_computation.1 | async-start | bytes 7454720 | tf_op jit(solution)/shard_map/all_gather | solution.py:68
  8.7 304.8 %all-gather.9.cloned.1.call-start = ((), (), s32[]{:S(2)}) async-start(), calls=%async_computation | async-start | bytes 7454720 | tf_op jit(solution)/shard_map/all_gather | solution.py:67
  9.4 390.9 %all-gather.15.cloned.1.call-start = ((), (), s32[]{:S(2)}) async-start(), calls=%async_computation.4 | async-start | bytes 34078720 | tf_op jit(solution)/shard_map/all_gather | solution.py:13
  12.4 305.4 %copy-start.7 = (bf16[128,128]{0,1:T(8,128)(2,1)}, bf16[128,128]{0,1:T(8,128)(2,1)S(1)}, u32[]{:S(2)}) copy-start(bf16[128,128]{0,1:T(8,128)(2,1)S(1)} %convolution_convert_fusion) | copy-start | bytes 98308
  12.4 87.4 %copy-start.4 = (bf16[2,64,1024]{2,1,0:T(8,128)(2,1)S(1)}, bf16[2,64,1024]{2,1,0:T(8,128)(2,1)}, u32[]{:S(2)}) copy-start(bf16[2,64,1024]{2,1,0:T(8,128)(2,1)} %param.17) | copy-start | bytes 786436
  100.0 82.8 %copy-start.9 = (u32[256]{0:T(256)S(1)}, u32[256]{0:T(256)}, u32[]{:S(2)}) copy-start(u32[256]{0:T(256)} %constant.80) | copy-start | bytes 3076
  100.0 212.0 %copy-start.6 = (bf16[128,1024]{1,0:T(8,128)(2,1)S(1)}, bf16[128,1024]{1,0:T(8,128)(2,1)}, u32[]{:S(2)}) copy-start(bf16[128,1024]{1,0:T(8,128)(2,1)} %param.19) | copy-start | bytes 786436
  181.2 138.9 %copy-start.1 = (bf16[128,1024]{1,0:T(8,128)(2,1)}, bf16[128,1024]{1,0:T(8,128)(2,1)S(1)}, u32[]{:S(2)}) copy-start(bf16[128,1024]{1,0:T(8,128)(2,1)S(1)} %multiply_convert_fusion) | copy-start | bytes 786436
  182.8 479.1 %all-gather.17.cloned.1.call-start = ((), (), s32[]{:S(2)}) async-start(), calls=%async_computation.5 | async-start | bytes 34078720 | tf_op jit(solution)/shard_map/all_gather | solution.py:13
  522.9 543.7 %all-reduce.7.cloned.1.call-start = ((), (), s32[]{:S(2)}) async-start(), calls=%async_computation.6 | async-start | bytes 3670016
  684.9 118.6 %copy-start.2 = (bf16[128,1024]{1,0:T(8,128)(2,1)S(1)}, bf16[128,1024]{1,0:T(8,128)(2,1)}, u32[]{:S(2)}) copy-start(bf16[128,1024]{1,0:T(8,128)(2,1)} %copy-done.1) | copy-start | bytes 786436
  684.9 119.2 %copy-start.3 = (bf16[8,128,128]{2,1,0:T(8,128)(2,1)S(1)}, bf16[8,128,128]{2,1,0:T(8,128)(2,1)}, u32[]{:S(2)}) copy-start(bf16[8,128,128]{2,1,0:T(8,128)(2,1)} %fusion.9) | copy-start | bytes 786436
  684.9 119.4 %copy-start.5 = (bf16[2,64,1024]{2,1,0:T(8,128)(2,1)S(1)}, bf16[2,64,1024]{2,1,0:T(8,128)(2,1)}, u32[]{:S(2)}) copy-start(bf16[2,64,1024]{2,1,0:T(8,128)(2,1)} %param.17) | copy-start | bytes 786436
  684.9 121.9 %copy-start.8 = (bf16[128,128]{0,1:T(8,128)(2,1)S(1)}, bf16[128,128]{0,1:T(8,128)(2,1)}, u32[]{:S(2)}) copy-start(bf16[128,128]{0,1:T(8,128)(2,1)} %copy-done.7) | copy-start | bytes 98308
  806.8 446.2 %all-reduce.5.cloned.1.call-start = ((), (), s32[]{:S(2)}) async-start(), calls=%async_computation.3 | async-start | bytes 1048576 | tf_op jit(solution)/shard_map/psum | solution.py:138
Sparse Core Ops, SparseCore 0:
  10.7 84.7 all-gather.12
  98.3 78.5 all-gather.10
  179.7 78.6 all-gather.8
  261.6 138.6 all-gather.14
  523.1 138.7 all-gather.16
  806.9 259.7 all-reduce.6
  1070.7 182.1 all-reduce.4
where the time goes:
time: 1270 us; the launch traced here: 1260 us
  waiting for transfers between devices  815 us (64%)
  other arithmetic  151 us (12%)
  blocking collectives  127 us (10%)
  local copies, waits for them, and re-layouts  119 us (9%)
  matrix products  30.3 us (2%)
  between operations  15 us (1%)
    unnamed x8, waiting for transfers between devices  260 us
    all_gather x2, waiting for transfers between devices, carried_in(): pieces = jax.tree.map(lambda part: lax.all_gather(part, axis), value)  210 us
    psum x1, waiting for transfers between devices, on_device(): grad_up = lax.psum(up_products, 'seq')  185 us
    select_n x126, other arithmetic, hop(): jnp.where(position < mine, new, old)  147 us
    unnamed x1, blocking collectives  127 us
    mul x126, local copies, waits for them, and re-layouts, combine(): later[0][:, None, None] * earlier[1] + later[1]  86.6 us
    all_gather x1, waiting for transfers between devices, on_device(): lax.all_gather(value_weight, 'seq', axis=0, tiled=True)  83.2 us
    all_gather x1, waiting for transfers between devices, on_device(): lax.all_gather(key_weight, 'seq', axis=0, tiled=True)  76.9 us
  transfers between devices with their start and end apart: 7, of which 6 were waited for; matrix products, arithmetic and copies ran while one was open for 3% of the time, Pallas kernels for 0%

commit v1 on v0

--- a/solution.py
+++ b/solution.py
@@ -66,7 +66,9 @@
     pieces = (
         lax.all_gather(query_weight, "seq", axis=0, tiled=True),
         lax.all_gather(key_weight, "seq", axis=0, tiled=True),
-        lax.all_gather(value_weight, "seq", axis=0, tiled=True),
+        jnp.concatenate(
+            lax.all_to_all(jnp.stack([value_weight] * lax.axis_size("seq")), "seq", 0, 0), axis=0
+        ),
     )
     columns = tokens
     query_frozen_part, key_base, value_frozen_part = tuple(

time: 1270 us -> 1250 us (0.984)
  waiting for transfers between devices: 815 us -> 777 us
    all_to_all x0 -> x1, waiting for transfers between devices: none -> 189 us  [on_device(): lax.all_to_all(jnp.stack([value_weight] * lax.axis_size('seq')), 'seq', 0...]
    all_gather x1 -> x0, waiting for transfers between devices: 83.2 us -> none  [on_device(): lax.all_gather(value_weight, 'seq', axis=0, tiled=True)]
    all_gather x1, waiting for transfers between devices: 76.9 us -> 0.02 us  [on_device(): lax.all_gather(key_weight, 'seq', axis=0, tiled=True)]
    all_gather x2, waiting for transfers between devices: 210 us -> 144 us  [carried_in(): pieces = jax.tree.map(lambda part: lax.all_gather(part, axis), value)]
    unnamed x8 -> x7, waiting for transfers between devices: 260 us -> 260 us
  transfers between devices with their start and end apart: 7 -> 7, of which waited for: 6 -> 5; matrix products, arithmetic and copies ran while one was open for 3% -> 3% of each run, Pallas kernels for 0% -> 0%
where the time goes in v1:
time: 1250 us; the launch traced here: 1240 us
  waiting for transfers between devices  777 us (62%)
  other arithmetic  150 us (12%)
  blocking collectives  130 us (10%)
  local copies, waits for them, and re-layouts  124 us (10%)
  matrix products  29.5 us (2%)
  between operations  15.1 us (1%)
  starting transfers between devices  12.9 us (1%)
    unnamed x7, waiting for transfers between devices  260 us
    all_to_all x1, waiting for transfers between devices, on_device(): lax.all_to_all(jnp.stack([value_weight] * lax.axis_size('seq')), 'seq', 0...  189 us
    psum x1, waiting for transfers between devices, on_device(): grad_up = lax.psum(up_products, 'seq')  184 us
    select_n x126, other arithmetic, hop(): jnp.where(position < mine, new, old)  147 us
    all_gather x2, waiting for transfers between devices, carried_in(): pieces = jax.tree.map(lambda part: lax.all_gather(part, axis), value)  144 us
    unnamed x1, blocking collectives  130 us
    mul x126, local copies, waits for them, and re-layouts, combine(): later[0][:, None, None] * earlier[1] + later[1]  86.6 us
  transfers between devices with their start and end apart: 7, of which 5 were waited for; matrix products, arithmetic and copies ran while one was open for 3% of the time, Pallas kernels for 0%

profile of v1, /device:TPU:2, one launch (start us, length us, event | category | flops | bytes accessed | tf_op | source)
XLA Modules:
  0.0 1241.8 jit_solution(1314748465940290323)
XLA Ops:
  7.9 4.8 stack.8
  12.7 12.5 %all-to-all-start = ((bf16[64,56,1024]{2,1,0:T(8,128)(2,1)}), bf16[64,56,1024]{2,1,0:T(8,128)(2,1)}, u32[]{:S(2)}, u32[]{:S(2)}) async-start(bf16[64,56,1024]{2,1,0:T(8,128)(2,1)} %stack.8), calls=%async_computation | async-start | bytes 14680064 | tf_op jit(solution)/shard_map/all_to_all | solution.py:70
  27.0 188.9 %all-to-all-done = bf16[64,56,1024]{2,1,0:T(8,128)(2,1)} async-done(((bf16[64,56,1024]{2,1,0:T(8,128)(2,1)}), bf16[64,56,1024]{2,1,0:T(8,128)(2,1)}, u32[]{:S(2)}, u32[]{:S(2)}) %all-to-all-start) | async-done | bytes 7340064 | tf_op jit(solution)/shard_map/all_to_all | solution.py:70
  215.9 4.3 fusion.57
  220.6 4.5 multiply_convert_fusion
  225.1 1.5 fusion.16
  228.3 130.4 %all-reduce = f32[512]{0:T(512)S(1)} all-reduce(f32[512]{0:T(512)S(1)} %dynamic-update-slice), channel_id=2, replica_groups=mesh['seq'=64,'mp'=4] {'seq'}, use_global_device_ids=true, to_apply=%add | all-reduce | flops 512 | bytes 4096
  360.1 4.2 fusion.56
  367.4 1.8 fusion.9
  369.2 12.3 all-gather.12.cloned.1.call-done
  381.5 118.0 %while.28 = (s32[]{:T(128)}, f32[8,128,128]{2,1,0:T(8,128)S(1)}, s32[]{:T(128)}, f32[64,8]{1,0:T(8,128)}, f32[64,8,128,128]{3,2,1,0:T(8,128)}, /*index=5*/s32[]{:T(128)}, s32[]{:T(128)}) while((s32[]{:T(128)}, f32[8,128,128]{2,1,0:T(8,128)S(1)}, s32[]{:T(128)}, f32[64,8]{1,0:T(8,128)}, f32[64,8,128,128]{3,2,1,0:T(8,128)}, ...), condition=%wide.region_2.3_spmd.clone, body=%wide.region_1.2_spmd.clone.sunk | while | flops 524292 | bytes 1573065 | solution.py:25
  500.1 1.4 multiply_reduce_fusion.1
  501.7 2.0 fusion.13
  503.9 1.4 rev.6
  506.9 1.3 fusion.2
  508.4 1.2 multiply_multiply_fusion
  509.7 1.3 fusion.36
  511.0 131.6 %all-gather.14.cloned.1.call-done = f32[512,128,128]{2,1,0:T(8,128)} async-done(((f32[8,128,128]{2,1,0:T(8,128)}), f32[512,128,128]{2,1,0:T(8,128)}) %all-gather.14.cloned.1.call-update) | async-done | bytes 33554448 | tf_op jit(solution)/shard_map/all_gather | solution.py:13
  642.6 23.0 %rev.7 = f32[64,8,128,128]{3,2,1,0:T(8,128)} reverse(f32[64,8,128,128]{3,2,1,0:T(8,128)} %bitcast.145), dimensions={0} | reverse | bytes 67108864 | tf_op jit(solution)/shard_map/rev | solution.py:15
  665.6 118.2 %while.29 = (s32[]{:T(128)}, f32[8,128,128]{2,1,0:T(8,128)S(1)}, s32[]{:T(128)}, f32[64,8]{1,0:T(8,128)}, f32[64,8,128,128]{3,2,1,0:T(8,128)}, /*index=5*/s32[]{:T(128)}, s32[]{:T(128)}) while((s32[]{:T(128)}, f32[8,128,128]{2,1,0:T(8,128)S(1)}, s32[]{:T(128)}, f32[64,8]{1,0:T(8,128)}, f32[64,8,128,128]{3,2,1,0:T(8,128)}, ...), condition=%wide.region_6.7_spmd.clone, body=%wide.region_5.6_spmd.clone.sunk | while | flops 524292 | bytes 1573065 | solution.py:25
  784.9 2.1 convolution_bitcast_fusion
  788.7 258.2 %all-reduce.7.cloned.1.call-done = f32[3584,128]{0,1:T(8,128)} async-done(((f32[3584,128]{0,1:T(8,128)}), f32[3584,128]{0,1:T(8,128)}) %all-reduce.7.cloned.1.call-update) | async-done | bytes 1835024
  1048.6 184.4 %all-reduce.5.cloned.1.call-done = f32[2,64,1024]{2,1,0:T(8,128)} async-done(((f32[2,64,1024]{2,1,0:T(8,128)}), f32[2,64,1024]{2,1,0:T(8,128)}) %all-reduce.5.cloned.1.call-update) | async-done | bytes 524304 | tf_op jit(solution)/shard_map/psum | solution.py:140
  1233.1 1.9 copy.120
  (322 shorter events, 249.4 us)
Async XLA Ops:
  7.2 19.4 %copy-start = (bf16[128,3584]{1,0:T(8,128)(2,1)S(1)}, bf16[128,3584]{1,0:T(8,128)(2,1)}, u32[]{:S(2)}) copy-start(bf16[128,3584]{1,0:T(8,128)(2,1)} %param.12) | copy-start | bytes 2752516
  7.2 213.4 %all-gather.10.cloned.1.call-start = ((), (), s32[]{:S(2)}) async-start(), calls=%async_computation.2 | async-start | bytes 7454720 | tf_op jit(solution)/shard_map/all_gather | solution.py:68
  12.7 13.3 %copy-start.10 = (f32[8,128]{1,0:T(8,128)S(1)}, f32[8,128]{1,0:T(8,128)}, u32[]{:S(2)}) copy-start(f32[8,128]{1,0:T(8,128)} %param.18) | copy-start | bytes 12292
  12.7 13.8 %copy-start.4 = (bf16[3584,128]{1,0:T(8,128)(2,1)S(1)}, bf16[3584,128]{1,0:T(8,128)(2,1)}, u32[]{:S(2)}) copy-start(bf16[3584,128]{1,0:T(8,128)(2,1)} %param.16) | copy-start | bytes 2752516
  12.7 203.3 %all-to-all-start = ((bf16[64,56,1024]{2,1,0:T(8,128)(2,1)}), bf16[64,56,1024]{2,1,0:T(8,128)(2,1)}, u32[]{:S(2)}, u32[]{:S(2)}) async-start(bf16[64,56,1024]{2,1,0:T(8,128)(2,1)} %stack.8), calls=%async_computation | async-start | bytes 14680064 | tf_op jit(solution)/shard_map/all_to_all | solution.py:70
  25.2 334.9 %all-gather.8.cloned.1.call-start = ((), (), s32[]{:S(2)}) async-start(), calls=%async_computation.1 | async-start | bytes 7454720 | tf_op jit(solution)/shard_map/all_gather | solution.py:67
  25.9 355.6 %all-gather.12.cloned.1.call-start = ((), (), s32[]{:S(2)}) async-start(), calls=%async_computation.4 | async-start | bytes 34078720 | tf_op jit(solution)/shard_map/all_gather | solution.py:13
  27.0 337.3 %copy-start.8 = (bf16[128,128]{0,1:T(8,128)(2,1)}, bf16[128,128]{0,1:T(8,128)(2,1)S(1)}, u32[]{:S(2)}) copy-start(bf16[128,128]{0,1:T(8,128)(2,1)S(1)} %convolution_convert_fusion) | copy-start | bytes 98308
  215.9 4.3 copy-start.5
  220.5 6.3 copy-start.11
  220.5 138.8 %copy-start.7 = (bf16[128,1024]{1,0:T(8,128)(2,1)S(1)}, bf16[128,1024]{1,0:T(8,128)(2,1)}, u32[]{:S(2)}) copy-start(bf16[128,1024]{1,0:T(8,128)(2,1)} %param.19) | copy-start | bytes 786436
  225.1 142.3 %copy-start.1 = (bf16[128,1024]{1,0:T(8,128)(2,1)}, bf16[128,1024]{1,0:T(8,128)(2,1)S(1)}, u32[]{:S(2)}) copy-start(bf16[128,1024]{1,0:T(8,128)(2,1)S(1)} %multiply_convert_fusion) | copy-start | bytes 786436
  226.7 415.9 %all-gather.14.cloned.1.call-start = ((), (), s32[]{:S(2)}) async-start(), calls=%async_computation.5 | async-start | bytes 34078720 | tf_op jit(solution)/shard_map/all_gather | solution.py:13
  503.7 543.3 %all-reduce.7.cloned.1.call-start = ((), (), s32[]{:S(2)}) async-start(), calls=%async_computation.6 | async-start | bytes 3670016
  665.6 118.2 %copy-start.2 = (bf16[128,1024]{1,0:T(8,128)(2,1)S(1)}, bf16[128,1024]{1,0:T(8,128)(2,1)}, u32[]{:S(2)}) copy-start(bf16[128,1024]{1,0:T(8,128)(2,1)} %copy-done.1) | copy-start | bytes 786436
  665.6 118.8 %copy-start.3 = (bf16[8,128,128]{2,1,0:T(8,128)(2,1)S(1)}, bf16[8,128,128]{2,1,0:T(8,128)(2,1)}, u32[]{:S(2)}) copy-start(bf16[8,128,128]{2,1,0:T(8,128)(2,1)} %fusion.9) | copy-start | bytes 786436
  665.6 119.0 %copy-start.6 = (bf16[2,64,1024]{2,1,0:T(8,128)(2,1)S(1)}, bf16[2,64,1024]{2,1,0:T(8,128)(2,1)}, u32[]{:S(2)}) copy-start(bf16[2,64,1024]{2,1,0:T(8,128)(2,1)} %param.17) | copy-start | bytes 786436
  665.6 121.6 %copy-start.9 = (bf16[128,128]{0,1:T(8,128)(2,1)S(1)}, bf16[128,128]{0,1:T(8,128)(2,1)}, u32[]{:S(2)}) copy-start(bf16[128,128]{0,1:T(8,128)(2,1)} %copy-done.8) | copy-start | bytes 98308
  787.1 446.0 %all-reduce.5.cloned.1.call-start = ((), (), s32[]{:S(2)}) async-start(), calls=%async_computation.3 | async-start | bytes 1048576 | tf_op jit(solution)/shard_map/psum | solution.py:140
Sparse Core Ops, SparseCore 0:
  10.7 127.7 all-gather.9
  141.3 96.0 all-gather.7
  240.7 140.8 all-gather.11
  503.8 138.7 all-gather.13
  787.2 259.7 all-reduce.6
  1050.9 182.1 all-reduce.4
